TPU v7x, 32 devices: a whole 2x2x4 slice. The times are simulated.
32 devices in a mesh: cuts: 4 (over z), blk: 2 (over x), rep: 4 (over y, core).
Axes of the slice: x: 2, y: 2, z: 4, core: 2. Of those that a mesh axis runs over, the one named last changes fastest.
Arguments:
- features: bfloat16 [8192, 256], P(('cuts', 'blk', 'rep')), may hold values from -6 to 6
- adj_values: bfloat16 [64, 4, 128, 1024], P(('cuts', 'blk'), 'rep'), as said below
- adj_cols: int32 [64, 4, 8], P(('cuts', 'blk'), 'rep'), may hold values from 0 to 15, as said below
- adj_count: int32 [64, 4], P(('cuts', 'blk'), 'rep'), may hold values from 1 to 8, as said below
- weight: bfloat16 [256, 256], replicated, may hold values from -0.375 to 0.375
- cotangent: bfloat16 [8192, 256], P(('cuts', 'blk', 'rep')), may hold values from -6 to 6
Outputs:
- output: bfloat16 [8192, 256], P(('cuts', 'blk', 'rep'))
- weight_grad: float32 [256, 256], replicated
Inputs may be any that keep to these rules, and one draw needn't show every extreme that they name: `adj_values`: entries are nonnegative; a row of a block has about 8 nonzero entries on average. `adj_cols`: within one row block and rep index the 8 numbers are distinct. `adj_count`: in every aligned group of 8 row blocks, for every rep index, some row block has count 8.
All inputs are finite; a program needn't handle non-finite values.
Results may differ from a plain program's by a relative error of at most 0.0061.
Values may be sent and summed in bfloat16 or wider, within the bound.
A program may use at most 64 MiB of HBM per device.

v0:
```python
import jax
import jax.numpy as jnp
from jax import lax
from jax.sharding import PartitionSpec as P


def silu_grad(pre):
    sigmoid_z = jax.nn.sigmoid(pre)
    return sigmoid_z * (1.0 + pre * (1.0 - sigmoid_z))


def local(features, adj_values, adj_cols, adj_count, weight, cotangent):
    block_size = adj_values.shape[2]
    slot_count = adj_cols.shape[2]
    feature_width = features.shape[1]
    group_rows = adj_values.shape[0]
    in_slice = lax.all_gather(features, "blk", axis=0, tiled=True)
    gathered = lax.all_gather(in_slice, "cuts", axis=0, tiled=True)
    panel_blocks = gathered.reshape(-1, block_size, feature_width)
    columns = adj_cols[:, 0, :]
    picked = panel_blocks[columns]
    slot_ids = jnp.arange(slot_count, dtype=jnp.int32)[None, :]
    usable = slot_ids < adj_count[:, 0][:, None]
    picked = jnp.where(usable[:, :, None, None], picked, jnp.zeros((), jnp.bfloat16))
    picked = picked.reshape(group_rows, slot_count * block_size, feature_width)
    partial_value = lax.dot_general(
        adj_values[:, 0], picked, (((2,), (1,)), ((0,), (0,))), preferred_element_type=jnp.float32
    )
    partial_value = partial_value.reshape(group_rows * block_size, feature_width)
    summed = lax.psum_scatter(partial_value, "rep", scatter_dimension=0, tiled=True)
    hidden = summed.astype(jnp.bfloat16)
    pre = jnp.dot(hidden, weight, preferred_element_type=jnp.float32)
    output = jax.nn.silu(pre).astype(jnp.bfloat16)
    grad_pre = (cotangent.astype(jnp.float32) * silu_grad(pre)).astype(jnp.bfloat16)
    local_grad = lax.dot_general(
        hidden, grad_pre, (((0,), (0,)), ((), ())), preferred_element_type=jnp.float32
    )
    weight_grad = lax.psum(local_grad, ("cuts", "blk", "rep"))
    return (output, weight_grad)


def solution(mesh):
    placed = (
        P(("cuts", "blk", "rep"), None),
        P(("cuts", "blk"), "rep", None, None),
        P(("cuts", "blk"), "rep", None),
        P(("cuts", "blk"), "rep"),
        P(),
        P(("cuts", "blk", "rep"), None),
    )
    return jax.shard_map(
        local,
        mesh=mesh,
        in_specs=placed,
        out_specs=(P(("cuts", "blk", "rep"), None), P()),
        check_vma=False,
    )
```

profile of v0, /device:TPU:0, one launch (start us, length us, event | category | flops | bytes accessed | tf_op | source)
XLA Modules:
  0.0 220.4 jit_solution(18052649329132863206)
XLA Ops:
  7.2 0.0 copy-start
  7.2 0.0 all-gather.2.cloned.1.call-start
  7.2 9.1 %all_gather.6 = bf16[512,256]{1,0:T(8,128)(2,1)} all-gather(bf16[256,256]{1,0:T(8,128)(2,1)} %param.6), channel_id=1, replica_groups=mesh['cuts'=4,'blk'=2,'rep'=4] {'blk'}, dimensions={0}, use_global_device_ids=true | all-gather | bytes 393216 | tf_op jit(solution)/shard_map/all_gather | solution.py:17
  16.4 0.0 all-gather.2.cloned.1.call-update
  16.4 0.0 reduce-scatter.2.cloned.1.call-start
  16.4 0.7 compare_select_fusion
  17.1 0.1 reshape.67
  17.2 0.7 iota_compare_fusion
  17.9 0.1 broadcast_bitcast_fusion
  18.0 26.9 %all-gather.2.cloned.1.call-done = bf16[2048,256]{1,0:T(8,128)(2,1)} async-done(((bf16[512,256]{1,0:T(8,128)(2,1)}), bf16[2048,256]{1,0:T(8,128)(2,1)}) %all-gather.2.cloned.1.call-update) | async-done | bytes 1048592 | tf_op jit(solution)/shard_map/all_gather | solution.py:18
  44.8 4.0 %gather_fusion = bf16[64,128,256]{2,1,0:T(8,128)(2,1)} fusion(bf16[16,128,256]{2,1,0:T(8,128)(2,1)} %bitcast.19, s32[1024]{0:T(1024)S(1)} %pad_clamp_fusion), kind=kCustom, calls=%fused_computation | custom fusion | bytes 8388864 | tf_op jit(solution)/shard_map/gather | solution.py:21
  48.8 4.6 %bitcast_select_fusion = bf16[8,1024,256]{2,1,0:T(8,128)(2,1)S(1)} fusion(pred[8,1024]{1,0:T(8,128)(4,1)S(1)} %broadcast_bitcast_fusion, bf16[8,1024,256]{2,1,0:T(8,128)(2,1)} %bitcast.18), kind=kLoop, calls=%fused_computation.1 | loop fusion | flops 2097152 | bytes 8396800 | tf_op jit(solution)/shard_map/jit(_where)/select_n | solution.py:24
  53.4 0.0 copy-done
  53.4 0.0 copy-start.1
  53.4 0.0 copy-start.2
  53.4 1.8 fusion
  55.2 0.0 reduce-scatter.2.cloned.1.call-update
  55.2 0.0 all-reduce.2.cloned.1.call-start
  55.3 24.2 %reduce-scatter.2.cloned.1.call-done = f32[256,256]{1,0:T(8,128)} async-done(((f32[1024,256]{1,0:T(8,128)}), f32[256,256]{1,0:T(8,128)}) %reduce-scatter.2.cloned.1.call-update) | async-done | bytes 262160 | tf_op jit(solution)/shard_map/reduce_scatter | solution.py:30
  79.5 0.0 copy-done.1
  79.5 1.8 multiply_convert_fusion.1
  81.4 0.0 copy-done.2
  81.4 1.9 fusion.2
  83.3 0.0 all-reduce.2.cloned.1.call-update
  83.3 128.8 %all-reduce.2.cloned.1.call-done = f32[256,256]{1,0:T(8,128)} async-done(((f32[256,256]{1,0:T(8,128)}), f32[256,256]{1,0:T(8,128)}) %all-reduce.2.cloned.1.call-update) | async-done | bytes 262160 | tf_op jit(solution)/shard_map/psum | solution.py:38
  212.2 1.7 copy.9
  (1 shorter events, 0.0 us)
Async XLA Ops:
  7.2 46.2 %copy-start = (bf16[8,1,128,1024]{3,2,1,0:T(8,128)(2,1)S(1)}, bf16[8,1,128,1024]{3,2,1,0:T(8,128)(2,1)}, u32[]{:S(2)}) copy-start(bf16[8,1,128,1024]{3,2,1,0:T(8,128)(2,1)} %param.7) | copy-start | bytes 6291460
  7.2 37.7 %all-gather.2.cloned.1.call-start = ((), (), s32[]{:S(2)}) async-start(), calls=%async_computation.1 | async-start | bytes 1310720 | tf_op jit(solution)/shard_map/all_gather | solution.py:18
  16.4 63.1 %reduce-scatter.2.cloned.1.call-start = ((), (), s32[]{:S(2)}) async-start(), calls=%async_computation.2 | async-start | bytes 1310720 | tf_op jit(solution)/shard_map/reduce_scatter | solution.py:30
  53.4 26.1 %copy-start.1 = (bf16[256,256]{1,0:T(8,128)(2,1)S(1)}, bf16[256,256]{1,0:T(8,128)(2,1)}, u32[]{:S(2)}) copy-start(bf16[256,256]{1,0:T(8,128)(2,1)} %param.10) | copy-start | bytes 393220
  53.4 27.9 %copy-start.2 = (bf16[256,256]{1,0:T(8,128)(2,1)S(1)}, bf16[256,256]{1,0:T(8,128)(2,1)}, u32[]{:S(2)}) copy-start(bf16[256,256]{1,0:T(8,128)(2,1)} %param.11) | copy-start | bytes 393220
  55.2 157.0 %all-reduce.2.cloned.1.call-start = ((), (), s32[]{:S(2)}) async-start(), calls=%async_computation.3 | async-start | bytes 524288 | tf_op jit(solution)/shard_map/psum | solution.py:38
Sparse Core Ops, SparseCore 0:
  16.5 28.2 all-gather.1
  55.3 24.1 reduce-scatter.1
  85.6 126.5 all-reduce.1
where the time goes:
time: 221 us; the launch traced here: 220 us
  waiting for transfers between devices  180 us (81%)
  between operations  13.8 us (6%)
  blocking collectives  9.13 us (4%)
  other arithmetic  5.95 us (3%)
  local copies, waits for them, and re-layouts  5.83 us (3%)
  matrix products  5.53 us (3%)
    psum x1, waiting for transfers between devices, local(): weight_grad = lax.psum(local_grad, ('cuts', 'blk', 'rep'))  129 us
    all_gather x1, waiting for transfers between devices, local(): gathered = lax.all_gather(in_slice, 'cuts', axis=0, tiled=True)  26.9 us
    reduce_scatter x1, waiting for transfers between devices, local(): lax.psum_scatter(partial_value, 'rep', scatter_dimension=0, tiled=True)  24.2 us
    all_gather x1, blocking collectives, local(): in_slice = lax.all_gather(features, 'blk', axis=0, tiled=True)  9.13 us
    select_n x1, other arithmetic, local(): jnp.where(usable[:, :, None, None], picked, jnp.zeros((), jnp.bfloat16))  4.58 us
  transfers between devices with their start and end apart: 3, of which 3 were waited for; matrix products, arithmetic and copies ran while one was open for 1% of the time, Pallas kernels for 0%

commit v1 on v0

--- a/solution.py
+++ b/solution.py
@@ -35,7 +35,7 @@
     local_grad = lax.dot_general(
         hidden, grad_pre, (((0,), (0,)), ((), ())), preferred_element_type=jnp.float32
     )
-    weight_grad = lax.psum(local_grad, ("cuts", "blk", "rep"))
+    weight_grad = lax.psum(lax.psum(local_grad, "cuts"), ("blk", "rep"))
     return (output, weight_grad)
 
 

time: 221 us -> 184 us (0.83)
  waiting for transfers between devices: 180 us -> 144 us
    psum x1 -> x2, waiting for transfers between devices: 129 us -> 92.4 us  [local(): weight_grad = lax.psum(lax.psum(local_grad, 'cuts'), ('blk', 'rep'))]
  transfers between devices with their start and end apart: 3 -> 4, of which waited for: 3 -> 4; matrix products, arithmetic and copies ran while one was open for 1% -> 1% of each run, Pallas kernels for 0% -> 0%
where the time goes in v1:
time: 184 us
  waiting for transfers between devices  144 us (78%)
  between operations  13.8 us (8%)
  blocking collectives  9.13 us (5%)
  other arithmetic  5.95 us (3%)
  local copies, waits for them, and re-layouts  5.83 us (3%)
  matrix products  5.53 us (3%)
    psum x2, waiting for transfers between devices, local(): weight_grad = lax.psum(lax.psum(local_grad, 'cuts'), ('blk', 'rep'))  92.4 us
    all_gather x1, waiting for transfers between devices, local(): gathered = lax.all_gather(in_slice, 'cuts', axis=0, tiled=True)  26.9 us
    reduce_scatter x1, waiting for transfers between devices, local(): lax.psum_scatter(partial_value, 'rep', scatter_dimension=0, tiled=True)  24.2 us
    all_gather x1, blocking collectives, local(): in_slice = lax.all_gather(features, 'blk', axis=0, tiled=True)  9.13 us
    select_n x1, other arithmetic, local(): jnp.where(usable[:, :, None, None], picked, jnp.zeros((), jnp.bfloat16))  4.58 us
    gather x1, local copies, waits for them, and re-layouts, local(): picked = panel_blocks[columns]  3.98 us
  transfers between devices with their start and end apart: 4, of which 4 were waited for; matrix products, arithmetic and copies ran while one was open for 1% of the time, Pallas kernels for 0%

profile of v1, /device:TPU:0, one launch (start us, length us, event | category | flops | bytes accessed | tf_op | source)
XLA Modules:
  0.0 184.0 jit_solution(17050339815561848411)
XLA Ops:
  7.2 0.0 copy-start
  7.2 0.0 all-gather.2.cloned.1.call-start
  7.2 9.1 %all_gather.6 = bf16[512,256]{1,0:T(8,128)(2,1)} all-gather(bf16[256,256]{1,0:T(8,128)(2,1)} %param.6), channel_id=1, replica_groups=mesh['cuts'=4,'blk'=2,'rep'=4] {'blk'}, dimensions={0}, use_global_device_ids=true | all-gather | bytes 393216 | tf_op jit(solution)/shard_map/all_gather | solution.py:17
  16.4 0.0 all-gather.2.cloned.1.call-update
  16.4 0.0 reduce-scatter.2.cloned.1.call-start
  16.4 0.7 compare_select_fusion
  17.1 0.1 reshape.67
  17.2 0.7 iota_compare_fusion
  17.9 0.1 broadcast_bitcast_fusion
  18.0 26.9 %all-gather.2.cloned.1.call-done = bf16[2048,256]{1,0:T(8,128)(2,1)} async-done(((bf16[512,256]{1,0:T(8,128)(2,1)}), bf16[2048,256]{1,0:T(8,128)(2,1)}) %all-gather.2.cloned.1.call-update) | async-done | bytes 1048592 | tf_op jit(solution)/shard_map/all_gather | solution.py:18
  44.8 4.0 %gather_fusion = bf16[64,128,256]{2,1,0:T(8,128)(2,1)} fusion(bf16[16,128,256]{2,1,0:T(8,128)(2,1)} %bitcast.19, s32[1024]{0:T(1024)S(1)} %pad_clamp_fusion), kind=kCustom, calls=%fused_computation | custom fusion | bytes 8388864 | tf_op jit(solution)/shard_map/gather | solution.py:21
  48.8 4.6 %bitcast_select_fusion = bf16[8,1024,256]{2,1,0:T(8,128)(2,1)S(1)} fusion(pred[8,1024]{1,0:T(8,128)(4,1)S(1)} %broadcast_bitcast_fusion, bf16[8,1024,256]{2,1,0:T(8,128)(2,1)} %bitcast.18), kind=kLoop, calls=%fused_computation.1 | loop fusion | flops 2097152 | bytes 8396800 | tf_op jit(solution)/shard_map/jit(_where)/select_n | solution.py:24
  53.4 0.0 copy-done
  53.4 0.0 copy-start.1
  53.4 0.0 copy-start.2
  53.4 1.8 fusion
  55.2 0.0 reduce-scatter.2.cloned.1.call-update
  55.2 0.0 all-reduce.3.cloned.1.call-start
  55.3 24.2 %reduce-scatter.2.cloned.1.call-done = f32[256,256]{1,0:T(8,128)} async-done(((f32[1024,256]{1,0:T(8,128)}), f32[256,256]{1,0:T(8,128)}) %reduce-scatter.2.cloned.1.call-update) | async-done | bytes 262160 | tf_op jit(solution)/shard_map/reduce_scatter | solution.py:30
  79.5 0.0 copy-done.1
  79.5 1.8 multiply_convert_fusion.1
  81.4 0.0 copy-done.2
  81.4 1.9 %fusion.2 = f32[256,256]{1,0:T(8,128)} fusion(f32[256,256]{1,0:T(8,128)S(1)} %get-tuple-element.3, bf16[256,256]{1,0:T(8,128)(2,1)S(1)} %copy-done.2, f32[256,256]{1,0:T(8,128)} %reduce-scatter.2.cloned.1.call-done), kind=kOutput, calls=%fused_computation.7 | convolution fusion | flops 34275328 | bytes 917504 | tf_op jit(solution)/shard_map/dot_general | solution.py:35
  83.3 0.0 all-reduce.3.cloned.1.call-update
  83.3 0.0 all-reduce.5.cloned.1.call-start
  83.4 35.7 %all-reduce.3.cloned.1.call-done = f32[256,256]{1,0:T(8,128)} async-done(((f32[256,256]{1,0:T(8,128)}), f32[256,256]{1,0:T(8,128)}) %all-reduce.3.cloned.1.call-update) | async-done | bytes 262160 | tf_op jit(solution)/shard_map/psum | solution.py:38
  119.1 0.0 all-reduce.5.cloned.1.call-update
  119.1 56.7 %all-reduce.5.cloned.1.call-done = f32[256,256]{1,0:T(8,128)} async-done(((f32[256,256]{1,0:T(8,128)}), f32[256,256]{1,0:T(8,128)}) %all-reduce.5.cloned.1.call-update) | async-done | bytes 262160 | tf_op jit(solution)/shard_map/psum | solution.py:38
  175.8 1.7 copy.10
  (1 shorter events, 0.0 us)
Async XLA Ops:
  7.2 46.2 %copy-start = (bf16[8,1,128,1024]{3,2,1,0:T(8,128)(2,1)S(1)}, bf16[8,1,128,1024]{3,2,1,0:T(8,128)(2,1)}, u32[]{:S(2)}) copy-start(bf16[8,1,128,1024]{3,2,1,0:T(8,128)(2,1)} %param.7) | copy-start | bytes 6291460
  7.2 37.7 %all-gather.2.cloned.1.call-start = ((), (), s32[]{:S(2)}) async-start(), calls=%async_computation.1 | async-start | bytes 1310720 | tf_op jit(solution)/shard_map/all_gather | solution.py:18
  16.4 63.1 %reduce-scatter.2.cloned.1.call-start = ((), (), s32[]{:S(2)}) async-start(), calls=%async_computation.2 | async-start | bytes 1310720 | tf_op jit(solution)/shard_map/reduce_scatter | solution.py:30
  53.4 26.1 %copy-start.1 = (bf16[256,256]{1,0:T(8,128)(2,1)S(1)}, bf16[256,256]{1,0:T(8,128)(2,1)}, u32[]{:S(2)}) copy-start(bf16[256,256]{1,0:T(8,128)(2,1)} %param.10) | copy-start | bytes 393220
  53.4 27.9 %copy-start.2 = (bf16[256,256]{1,0:T(8,128)(2,1)S(1)}, bf16[256,256]{1,0:T(8,128)(2,1)}, u32[]{:S(2)}) copy-start(bf16[256,256]{1,0:T(8,128)(2,1)} %param.11) | copy-start | bytes 393220
  55.2 63.9 %all-reduce.3.cloned.1.call-start = ((), (), s32[]{:S(2)}) async-start(), calls=%async_computation.3 | async-start | bytes 524288 | tf_op jit(solution)/shard_map/psum | solution.py:38
  83.3 92.4 %all-reduce.5.cloned.1.call-start = ((), (), s32[]{:S(2)}) async-start(), calls=%async_computation.4 | async-start | bytes 524288 | tf_op jit(solution)/shard_map/psum | solution.py:38
Sparse Core Ops, SparseCore 0:
  16.5 28.2 all-gather.1
  55.3 24.1 reduce-scatter.1
  83.4 35.5 all-reduce.2
  122.0 53.7 all-reduce.4
